TPU v7x, 32 devices: a whole 2x2x4 slice. The times are simulated.
32 devices in a mesh: parts: 2 (over x), dp: 4 (over y, core), shard: 4 (over z).
Axes of the slice: x: 2, y: 2, z: 4, core: 2. Of those that a mesh axis runs over, the one named last changes fastest.
Arguments:
- projected: bfloat16 [7680, 7680], P(('parts', 'dp', 'shard')), parts along dimension 0, may hold values from -4 to 4
- residual: bfloat16 [7680, 2560], P(('parts', 'dp', 'shard')), parts along dimension 0, may hold values from -6 to 6
- out_weight: bfloat16 [2560, 2560], P(None, 'shard'), may hold values from -0.125 to 0.125
- probe_weight: bfloat16 [2, 2560, 8], replicated, may hold values from -0.125 to 0.125
- labels: int32 [7680], P(('parts', 'dp', 'shard')), parts along dimension 0, may hold values from 0 to 7
- lengths: int32 [32, 9], P(('parts', 'dp', 'shard')), parts along dimension 0, may hold values from 12 to 48, as said below
- destination: int32 [32, 9], P(('parts', 'dp', 'shard')), parts along dimension 0, may hold values from 0 to 3, as said below
Outputs:
- hidden_rows: bfloat16 [18432, 2560], P(('parts', 'dp', 'shard')), parts along dimension 0
- probe_grad: float32 [4, 2560, 8], P('parts'), parts along dimension 0
There are 2 independent parts, one for each index of `parts`. A program takes and returns all parts, laid end to end along the dimension named above; an argument that names none is the same for every part. Nothing has to cross between parts.
Inputs may be any that keep to these rules, and one draw needn't show every extreme that they name: Each row of lengths sums to 240 and holds exactly one protein of length 48. `destination`: A loader assigns at most 3 proteins to any one dp index; in every shard column one dp index is assigned exactly 3 proteins by every loader of that column.
All inputs are finite; a program needn't handle non-finite values.
Results may differ from a plain program's by a relative error of at most 0.0031.
Values may be sent and summed in bfloat16 or wider, within the bound.
No kernel may reach another device: no remote copies, remote signals or barrier semaphores. Data moves between devices by JAX's collectives and lax.ppermute only.
A program may use at most 128 MiB of HBM per device.

v0:
```python
import jax
import jax.numpy as jnp
from jax import lax
from jax.sharding import PartitionSpec as P

HS = 128
CLASSES = 8
LMAX = 48
TOK_DEV = 240


def attend(blocks, block_lengths):
    block_count = blocks.shape[0]
    span_rows = blocks.shape[1]
    head_width = blocks.shape[2] // 3
    head_count = head_width // HS
    queries = blocks[:, :, :head_width].reshape(block_count, span_rows, head_count, HS)
    key_rows = blocks[:, :, head_width : 2 * head_width].reshape(
        block_count, span_rows, head_count, HS
    )
    value_rows = blocks[:, :, 2 * head_width :].reshape(block_count, span_rows, head_count, HS)
    scores = jnp.einsum(
        "plhs,pmhs->phlm", queries, key_rows, preferred_element_type=jnp.float32
    ) * HS ** (-0.5)
    keep_mask = (jnp.arange(span_rows, dtype=jnp.int32)[None, :] < block_lengths[:, None]).astype(
        jnp.float32
    )
    weights = jnp.exp(scores) * keep_mask[:, None, None, :]
    denominator = (
        jnp.sum(weights, axis=-1, keepdims=True)
        + (block_lengths == 0).astype(jnp.float32)[:, None, None, None]
    )
    weight_low = (weights / denominator).astype(jnp.bfloat16)
    attended = jnp.einsum(
        "phlm,pmhs->plhs", weight_low, value_rows, preferred_element_type=jnp.float32
    )
    return attended.reshape(block_count * span_rows, head_width).astype(jnp.bfloat16)


def project(attended, out_weight):
    return jnp.dot(
        attended,
        lax.all_gather(out_weight, "shard", axis=1, tiled=True),
        preferred_element_type=jnp.float32,
    )


def probe_terms(represent_x, represent_h, label_rows, keep_mask, probe_weight):
    one_hot = (label_rows[:, None] == jnp.arange(CLASSES, dtype=jnp.int32)[None, :]).astype(
        jnp.float32
    )
    collected = []
    for which, represent in enumerate((represent_x, represent_h)):
        logits = jnp.dot(represent, probe_weight[which], preferred_element_type=jnp.float32)
        exponent = jnp.exp(logits)
        likelihood = exponent / jnp.sum(exponent, axis=1, keepdims=True)
        mismatch = ((likelihood - one_hot) * keep_mask[:, None] / TOK_DEV).astype(jnp.bfloat16)
        collected.append(
            lax.dot_general(
                represent, mismatch, (((0,), (0,)), ((), ())), preferred_element_type=jnp.float32
            )
        )
    return jnp.stack(collected)


def per_device(projected, residual, out_weight, probe_weight, labels, lengths, destination):
    group_size = lax.axis_size("dp")
    prot_count = lengths.shape[1]
    slot_count = -(-prot_count // group_size)
    tok_count = projected.shape[0]
    lens_own = lengths[0]
    dest_own = destination[0]
    starts = jnp.cumsum(lens_own) - lens_own
    offsets = jnp.arange(LMAX, dtype=jnp.int32)
    positions = jnp.arange(prot_count, dtype=jnp.int32)
    same_dest = dest_own[:, None] == dest_own[None, :]
    earlier = positions[:, None] > positions[None, :]
    slot_rank = jnp.sum((same_dest & earlier).astype(jnp.int32), axis=1)
    slot_match = (
        dest_own[None, None, :] == jnp.arange(group_size, dtype=jnp.int32)[:, None, None]
    ) & (slot_rank[None, None, :] == jnp.arange(slot_count, dtype=jnp.int32)[None, :, None])
    match_int = slot_match.astype(jnp.int32)
    slot_start = jnp.sum(match_int * starts, axis=2)
    slot_len = jnp.sum(match_int * lens_own, axis=2)
    block_count = group_size * slot_count
    row_index = jnp.minimum(slot_start[:, :, None] + offsets, tok_count - 1).reshape(
        group_size, slot_count * LMAX
    )
    live_rows = (offsets[None, None, :] < slot_len[:, :, None]).reshape(
        group_size, slot_count * LMAX
    )
    rows_send = jnp.where(live_rows[:, :, None], jnp.take(projected, row_index, axis=0), 0)
    resid_send = jnp.where(live_rows[:, :, None], jnp.take(residual, row_index, axis=0), 0)
    label_send = jnp.where(live_rows, jnp.take(labels, row_index), 0)
    got_labels, got_lengths = (
        lax.all_to_all(label_send, "dp", split_axis=0, concat_axis=0, tiled=True),
        lax.all_to_all(slot_len, "dp", split_axis=0, concat_axis=0, tiled=True),
    )
    got_rows, got_resid = (
        lax.all_to_all(rows_send, "dp", split_axis=0, concat_axis=0, tiled=True),
        lax.all_to_all(resid_send, "dp", split_axis=0, concat_axis=0, tiled=True),
    )
    lengths_recv = got_lengths.reshape(block_count)
    attended = attend(got_rows.reshape(block_count, LMAX, -1), lengths_recv)
    keep_mask = (offsets[None, :] < lengths_recv[:, None]).astype(jnp.float32).reshape(-1)
    represent = got_resid.reshape(block_count * LMAX, -1)
    mixed_rows = project(attended, out_weight) + represent.astype(jnp.float32)
    hidden = (mixed_rows * keep_mask[:, None]).astype(jnp.bfloat16)
    grad_terms = probe_terms(represent, hidden, got_labels.reshape(-1), keep_mask, probe_weight)
    grad_sum = lax.psum(grad_terms, ("dp", "shard"))
    return (hidden, grad_sum)


def solution(mesh):
    return jax.shard_map(
        per_device,
        mesh=mesh,
        in_specs=(
            P(("parts", "dp", "shard"), None),
            P(("parts", "dp", "shard"), None),
            P(None, "shard"),
            P(),
            P(("parts", "dp", "shard")),
            P(("parts", "dp", "shard"), None),
            P(("parts", "dp", "shard"), None),
        ),
        out_specs=(P(("parts", "dp", "shard"), None), P("parts", None, None)),
        check_vma=False,
    )
```

profile of v0, /device:TPU:8, one launch (start us, length us, event | category | flops | bytes accessed | tf_op | source)
XLA Modules:
  0.0 349.7 jit_solution(5877579920904036037)
XLA Ops:
  7.2 0.0 copy-start
  7.2 0.0 copy-start.5
  7.2 0.0 copy-start.6
  7.2 0.0 all-gather.2.cloned.1.call-start
  7.2 0.7 all-gather.2.cloned.1.call-update
  7.9 0.2 reduce-window.8
  8.1 0.2 convert_reduce_fusion
  8.3 0.2 fusion.37
  8.5 0.7 copy.27
  9.2 3.2 all-to-all-start.1
  12.4 0.1 copy.22
  12.5 0.1 copy.23
  12.6 0.1 add.96
  12.7 0.1 add.97
  12.8 0.1 add.101
  12.8 0.1 add.108
  12.9 0.1 lt.133
  13.0 0.1 lt.134
  13.1 0.1 lt.146
  13.2 0.1 lt.131
  13.3 0.1 reshape.363
  13.4 0.0 copy-start.2
  13.4 4.2 %gather_fusion.1 = bf16[576,2560]{1,0:T(8,128)(2,1)} fusion(bf16[240,2560]{1,0:T(8,128)(2,1)S(1)} %copy-done, s32[1024]{0:T(1024)S(1)} %pad_clamp_fusion), kind=kCustom, calls=%fused_computation.1 | custom fusion | bytes 5900544 | tf_op jit(solution)/shard_map/jit(_take)/gather | solution.py:93
  17.6 0.0 copy-done.2
  17.6 3.9 %gather_fusion.2 = s32[576]{0:T(1024)S(1)} fusion(s32[240]{0:T(256)S(1)} %copy-done.2, s32[1024]{0:T(1024)S(1)} %pad_clamp_fusion), kind=kCustom, calls=%fused_computation.2 | custom fusion | bytes 6912 | tf_op jit(solution)/shard_map/jit(_take)/gather | solution.py:94
  21.5 0.1 gather.17
  21.6 0.6 copy.31
  22.2 0.0 all-to-all-done.1
  22.3 3.3 all-to-all-start.3
  25.5 4.2 %select_select_fusion.1 = bf16[4,144,2560]{2,1,0:T(8,128)(2,1)} fusion(bf16[4,144,2560]{2,1,0:T(8,128)(2,1)} %bitcast.61, pred[4,144]{1,0:T(4,128)(4,1)S(1)} %get-tuple-element.8, pred[4,144]{1,0:T(4,128)(4,1)S(1)} %get-tuple-element.7), kind=kLoop, calls=%fused_computation.23 | loop fusion | flops 2949120 | bytes 5899392 | tf_op jit(solution)/shard_map/jit(_where)/select_n | solution.py:93
  29.7 22.4 %gather_fusion = bf16[576,7680]{1,0:T(8,128)(2,1)} fusion(bf16[240,7680]{1,0:T(8,128)(2,1)} %param.7, s32[1024]{0:T(1024)S(1)} %pad_clamp_fusion), kind=kCustom, calls=%fused_computation | custom fusion | bytes 17697024 | tf_op jit(solution)/shard_map/jit(_take)/gather | solution.py:92
  52.1 0.0 all-to-all-done.3
  52.1 4.6 %all-to-all-start.2 = ((bf16[4,144,2560]{2,1,0:T(8,128)(2,1)}), bf16[4,144,2560]{2,1,0:T(8,128)(2,1)}, u32[]{:S(2)}, u32[]{:S(2)}) async-start(bf16[4,144,2560]{2,1,0:T(8,128)(2,1)} %select_select_fusion.1), calls=%async_computation.2 | async-start | bytes 5898240 | tf_op jit(solution)/shard_map/all_to_all | solution.py:101
  56.8 8.1 %select_select_fusion = bf16[4,144,7680]{2,1,0:T(8,128)(2,1)} fusion(bf16[4,144,7680]{2,1,0:T(8,128)(2,1)} %bitcast.60, pred[4,144]{1,0:T(4,128)(4,1)S(1)} %get-tuple-element.8, pred[4,144]{1,0:T(4,128)(4,1)S(1)} %get-tuple-element.7), kind=kLoop, calls=%fused_computation.3 | loop fusion | flops 8847360 | bytes 17695872 | tf_op jit(solution)/shard_map/jit(_where)/select_n | solution.py:92
  64.9 26.7 %all-to-all-done.2 = bf16[4,144,2560]{2,1,0:T(8,128)(2,1)} async-done(((bf16[4,144,2560]{2,1,0:T(8,128)(2,1)}), bf16[4,144,2560]{2,1,0:T(8,128)(2,1)}, u32[]{:S(2)}, u32[]{:S(2)}) %all-to-all-start.2) | async-done | bytes 2949152 | tf_op jit(solution)/shard_map/all_to_all | solution.py:101
  91.6 5.7 %all-to-all-start = ((bf16[4,144,7680]{2,1,0:T(8,128)(2,1)}), bf16[4,144,7680]{2,1,0:T(8,128)(2,1)}, u32[]{:S(2)}, u32[]{:S(2)}) async-start(bf16[4,144,7680]{2,1,0:T(8,128)(2,1)} %select_select_fusion), calls=%async_computation | async-start | bytes 17694720 | tf_op jit(solution)/shard_map/all_to_all | solution.py:100
  97.3 0.2 all-reduce.2.cloned.1.call-start
  97.6 0.5 broadcast.237
  98.1 0.7 reduce.4
  98.7 0.1 lt.142
  98.8 0.1 fusion.36
  98.9 0.1 reshape.360
  99.0 0.1 eq.84
  99.1 0.0 copy-done.4
  99.1 2.7 fusion.43
  101.8 2.3 convolution_bitcast_fusion.1
  104.1 91.3 %all-to-all-done = bf16[4,144,7680]{2,1,0:T(8,128)(2,1)} async-done(((bf16[4,144,7680]{2,1,0:T(8,128)(2,1)}), bf16[4,144,7680]{2,1,0:T(8,128)(2,1)}, u32[]{:S(2)}, u32[]{:S(2)}) %all-to-all-start) | async-done | bytes 8847392 | tf_op jit(solution)/shard_map/all_to_all | solution.py:100
  195.4 4.0 %slice_bitcast_fusion.2 = (bf16[12,6,20,8,128]{4,3,2,1,0:T(8,128)(2,1)S(1)}, bf16[12,6,20,8,128]{4,3,2,1,0:T(8,128)(2,1)S(1)}, bf16[12,6,20,8,128]{4,3,2,1,0:T(8,128)(2,1)S(1)}) fusion(bf16[12,48,7680]{2,1,0:T(8,128)(2,1)} %bitcast.5), kind=kLoop, calls=%fused_computation.22 | loop fusion | bytes 17694720
  199.4 1.7 fusion
  201.1 0.1 broadcast_add_fusion
  201.2 2.0 convert_bitcast_fusion
  203.2 2.6 copy.30
  205.8 28.8 %all-gather.2.cloned.1.call-done = bf16[2560,2560]{1,0:T(8,128)(2,1)} async-done(((bf16[2560,640]{1,0:T(8,128)(2,1)}), bf16[2560,2560]{1,0:T(8,128)(2,1)}) %all-gather.2.cloned.1.call-update) | async-done | bytes 13107216 | tf_op jit(solution)/shard_map/all_gather | solution.py:43
  234.6 12.4 %multiply_convert_fusion = bf16[576,2560]{1,0:T(8,128)(2,1)S(1)} fusion(bf16[576,2560]{1,0:T(8,128)(2,1)} %bitcast.9, bf16[2560,2560]{1,0:T(8,128)(2,1)} %all-gather.2.cloned.1.call-done, bf16[72,8,20,128]{3,2,1,0:T(8,128)(2,1)} %bitcast.62, f32[576]{0:T(1024)S(1)} %reshape.360), kind=kOutput, calls=%fused_computation.4 | convolution fusion | flops 7555645440 | bytes 21956864 | tf_op jit(solution)/shard_map/dot_general | solution.py:41
  246.9 0.0 copy-start.3
  246.9 0.9 fusion.42
  247.8 0.0 copy-start.1
  247.8 0.5 convolution_bitcast_fusion
  248.3 0.2 copy-done.3
  248.5 0.7 pad_maximum_fusion
  249.2 0.0 all-reduce.2.cloned.1.call-update
  249.2 92.0 %all-reduce.2.cloned.1.call-done = f32[2,2560,8]{1,2,0:T(8,128)} async-done(((f32[2,2560,8]{1,2,0:T(8,128)}), f32[2,2560,8]{1,2,0:T(8,128)}) %all-reduce.2.cloned.1.call-update) | async-done | bytes 163856 | tf_op jit(solution)/shard_map/psum | solution.py:110
  341.3 1.6 copy.62
  342.9 0.0 copy-done.1
  (14 shorter events, 0.1 us)
Async XLA Ops:
  7.2 6.2 %copy-start = (bf16[240,2560]{1,0:T(8,128)(2,1)S(1)}, bf16[240,2560]{1,0:T(8,128)(2,1)}, u32[]{:S(2)}) copy-start(bf16[240,2560]{1,0:T(8,128)(2,1)} %param.8) | copy-start | bytes 3686404
  7.2 0.8 copy-start.5
  7.2 0.9 copy-start.6
  7.2 227.4 %all-gather.2.cloned.1.call-start = ((), (), s32[]{:S(2)}) async-start(), calls=%async_computation.4 | async-start | bytes 16384000 | tf_op jit(solution)/shard_map/all_gather | solution.py:43
  9.2 13.1 %all-to-all-start.1 = ((s32[4,1,3]{2,1,0:T(1,128)}), s32[4,1,3]{2,1,0:T(1,128)S(1)}, u32[]{:S(2)}, u32[]{:S(2)}) async-start(s32[4,1,3]{2,1,0:T(1,128)} %copy.27), calls=%async_computation.1 | async-start | bytes 4096 | tf_op jit(solution)/shard_map/all_to_all | solution.py:97
  13.4 4.2 %copy-start.2 = (s32[240]{0:T(256)S(1)}, s32[240]{0:T(256)}, u32[]{:S(2)}) copy-start(s32[240]{0:T(256)} %param.11) | copy-start | bytes 2884
  22.3 29.9 %all-to-all-start.3 = ((s32[4,1,144]{2,1,0:T(1,128)}), s32[4,1,144]{2,1,0:T(1,128)S(1)}, u32[]{:S(2)}, u32[]{:S(2)}) async-start(s32[4,1,144]{2,1,0:T(1,128)} %copy.31), calls=%async_computation.3 | async-start | bytes 8192 | tf_op jit(solution)/shard_map/all_to_all | solution.py:96
  52.1 39.5 %all-to-all-start.2 = ((bf16[4,144,2560]{2,1,0:T(8,128)(2,1)}), bf16[4,144,2560]{2,1,0:T(8,128)(2,1)}, u32[]{:S(2)}, u32[]{:S(2)}) async-start(bf16[4,144,2560]{2,1,0:T(8,128)(2,1)} %select_select_fusion.1), calls=%async_computation.2 | async-start | bytes 5898240 | tf_op jit(solution)/shard_map/all_to_all | solution.py:101
  64.9 34.2 %copy-start.4 = (bf16[2,2560,8]{1,2,0:T(8,128)(2,1)S(1)}, bf16[2,2560,8]{1,2,0:T(8,128)(2,1)}, u32[]{:S(2)}) copy-start(bf16[2,2560,8]{1,2,0:T(8,128)(2,1)} %param.10) | copy-start | bytes 245764
  91.6 103.8 %all-to-all-start = ((bf16[4,144,7680]{2,1,0:T(8,128)(2,1)}), bf16[4,144,7680]{2,1,0:T(8,128)(2,1)}, u32[]{:S(2)}, u32[]{:S(2)}) async-start(bf16[4,144,7680]{2,1,0:T(8,128)(2,1)} %select_select_fusion), calls=%async_computation | async-start | bytes 17694720 | tf_op jit(solution)/shard_map/all_to_all | solution.py:100
  97.3 244.0 %all-reduce.2.cloned.1.call-start = ((), (), s32[]{:S(2)}) async-start(), calls=%async_computation.5 | async-start | bytes 327680 | tf_op jit(solution)/shard_map/psum | solution.py:110
  246.9 1.6 copy-start.3
  247.8 95.0 %copy-start.1 = (bf16[240,2560]{1,0:T(8,128)(2,1)S(1)}, bf16[240,2560]{1,0:T(8,128)(2,1)}, u32[]{:S(2)}) copy-start(bf16[240,2560]{1,0:T(8,128)(2,1)} %param.8) | copy-start | bytes 3686404
Sparse Core Ops, SparseCore 0:
  9.6 224.9 all-gather.1
  249.4 91.8 all-reduce.1
where the time goes:
time: 350 us
  waiting for transfers between devices  239 us (68%)
  local copies, waits for them, and re-layouts  42 us (12%)
  matrix products  22.5 us (6%)
  starting transfers between devices  17 us (5%)
  other arithmetic  14.4 us (4%)
  between operations  14.3 us (4%)
    psum x1, waiting for transfers between devices, per_device(): grad_sum = lax.psum(grad_terms, ('dp', 'shard'))  92 us
    all_to_all x1, waiting for transfers between devices, per_device(): lax.all_to_all(rows_send, 'dp', split_axis=0, concat_axis=0, tiled=True)  91.3 us
    all_gather x1, waiting for transfers between devices, project(): lax.all_gather(out_weight, 'shard', axis=1, tiled=True)  28.8 us
    all_to_all x1, waiting for transfers between devices, per_device(): lax.all_to_all(resid_send, 'dp', split_axis=0, concat_axis=0, tiled=True)  26.7 us
    gather x1, local copies, waits for them, and re-layouts, per_device(): jnp.take(projected, row_index, axis=0)  22.4 us
    dot_general x1, matrix products, project(): jnp.dot(attended, lax.all_gather(out_weight, 'shard', axis=1, tiled=True)...  12.4 us
    select_n x1, other arithmetic, per_device(): jnp.where(live_rows[:, :, None], jnp.take(projected, row_index, axis=0), 0)  8.14 us
  transfers between devices with their start and end apart: 6, of which 4 were waited for; matrix products, arithmetic and copies ran while one was open for 18% of the time, Pallas kernels for 0%

commit v1 on v0

--- a/solution.py
+++ b/solution.py
@@ -7,6 +7,29 @@
 CLASSES = 8
 LMAX = 48
 TOK_DEV = 240
+
+
+def in_blocks(x, dim, devices):
+    before, after = (x.shape[:dim], x.shape[dim + 1 :])
+    return jnp.moveaxis(x.reshape(*before, devices, -1, *after), dim, 0)
+
+
+def laid_out(tiles, dim):
+    dims = list(tiles.shape[1:])
+    dims[dim] *= tiles.shape[0]
+    return jnp.moveaxis(tiles, 0, dim).reshape(dims)
+
+
+def exchange_directly(x, axis, split_dim, concat_dim):
+    devices, here = (lax.axis_size(axis), lax.axis_index(axis))
+    pieces = in_blocks(x, split_dim, devices)
+    result = pieces
+    for step in range(1, devices):
+        target, source = ((here + step) % devices, (here - step) % devices)
+        sent = lax.dynamic_index_in_dim(pieces, target, 0)
+        theirs = lax.ppermute(sent, axis, [(i, (i + step) % devices) for i in range(devices)])
+        result = lax.dynamic_update_slice_in_dim(result, theirs, source, axis=0)
+    return laid_out(result, concat_dim)
 
 
 def attend(blocks, block_lengths):
@@ -98,7 +121,7 @@
     )
     got_rows, got_resid = (
         lax.all_to_all(rows_send, "dp", split_axis=0, concat_axis=0, tiled=True),
-        lax.all_to_all(resid_send, "dp", split_axis=0, concat_axis=0, tiled=True),
+        exchange_directly(resid_send, "dp", 0, 0),
     )
     lengths_recv = got_lengths.reshape(block_count)
     attended = attend(got_rows.reshape(block_count, LMAX, -1), lengths_recv)

time: 350 us -> 350 us (level)
  local copies, waits for them, and re-layouts: 42 us -> 47.9 us
    ppermute x0 -> x3, waiting for transfers between devices: none -> 110 us  [exchange_directly(): lax.ppermute(sent, axis, [(i, (i + step) % devices) for i in range(device...]
    all_to_all x1, waiting for transfers between devices: 91.3 us -> 0.01 us  [per_device(): lax.all_to_all(rows_send, 'dp', split_axis=0, concat_axis=0, tiled=True)]
    all_to_all x1 -> x0, waiting for transfers between devices: 26.7 us -> none  [per_device(): lax.all_to_all(resid_send, 'dp', split_axis=0, concat_axis=0, tiled=True)]
    all_gather x1, waiting for transfers between devices: 28.8 us -> 34.1 us  [project(): lax.all_gather(out_weight, 'shard', axis=1, tiled=True)]
    dynamic_update_slice x0 -> x3, local copies, waits for them, and re-layouts: none -> 4.96 us  [exchange_directly(): result = lax.dynamic_update_slice_in_dim(result, theirs, source, axis=0)]
    all_to_all x1 -> x0, starting transfers between devices: 4.61 us -> none  [per_device(): lax.all_to_all(resid_send, 'dp', split_axis=0, concat_axis=0, tiled=True)]
  transfers between devices with their start and end apart: 6 -> 8, of which waited for: 4 -> 4; matrix products, arithmetic and copies ran while one was open for 18% -> 19% of each run, Pallas kernels for 0% -> 0%
where the time goes in v1:
time: 350 us
  waiting for transfers between devices  237 us (68%)
  local copies, waits for them, and re-layouts  47.9 us (14%)
  matrix products  20.7 us (6%)
  starting transfers between devices  15.8 us (5%)
  other arithmetic  14.5 us (4%)
  between operations  14.3 us (4%)
    ppermute x3, waiting for transfers between devices, exchange_directly(): lax.ppermute(sent, axis, [(i, (i + step) % devices) for i in range(device...  110 us
    psum x1, waiting for transfers between devices, per_device(): grad_sum = lax.psum(grad_terms, ('dp', 'shard'))  92.1 us
    all_gather x1, waiting for transfers between devices, project(): lax.all_gather(out_weight, 'shard', axis=1, tiled=True)  34.1 us
    gather x1, local copies, waits for them, and re-layouts, per_device(): jnp.take(projected, row_index, axis=0)  23.1 us
    dot_general x1, matrix products, project(): jnp.dot(attended, lax.all_gather(out_weight, 'shard', axis=1, tiled=True)...  12.3 us
    select_n x1, other arithmetic, per_device(): jnp.where(live_rows[:, :, None], jnp.take(projected, row_index, axis=0), 0)  8.04 us
  transfers between devices with their start and end apart: 8, of which 4 were waited for; matrix products, arithmetic and copies ran while one was open for 19% of the time, Pallas kernels for 0%

profile of v1, /device:TPU:8, one launch (start us, length us, event | category | flops | bytes accessed | tf_op | source)
XLA Modules:
  0.0 349.7 jit_solution(5329340811306819259)
XLA Ops:
  7.2 0.0 copy-start
  7.2 0.0 all-gather.2.cloned.1.call-start
  7.3 0.7 all-gather.2.cloned.1.call-update
  8.0 0.2 reduce-window.8
  8.1 0.2 convert_reduce_fusion
  8.4 0.2 fusion.40
  8.5 0.7 copy.27
  9.2 3.2 all-to-all-start.1
  12.4 0.1 copy.22
  12.5 0.1 copy.23
  12.6 0.1 add.146
  12.7 0.1 add.147
  12.8 0.1 add.151
  12.9 0.1 add.173
  13.0 0.1 lt.178
  13.0 0.1 lt.179
  13.1 0.1 lt.203
  13.2 0.1 lt.176
  13.3 0.1 reshape.373
  13.4 3.9 %gather_fusion.2 = s32[576]{0:T(1024)S(1)} fusion(s32[240]{0:T(256)S(1)} %copy-done.2, s32[1024]{0:T(1024)S(1)} %pad_clamp_fusion), kind=kCustom, calls=%fused_computation.2 | custom fusion | bytes 6912 | tf_op jit(solution)/shard_map/jit(_take)/gather | solution.py:117
  17.4 0.1 gather.20
  17.5 0.6 copy.31
  18.1 23.1 %gather_fusion = bf16[576,7680]{1,0:T(8,128)(2,1)} fusion(bf16[240,7680]{1,0:T(8,128)(2,1)} %param.7, s32[1024]{0:T(1024)S(1)} %pad_clamp_fusion), kind=kCustom, calls=%fused_computation | custom fusion | bytes 17697024 | tf_op jit(solution)/shard_map/jit(_take)/gather | solution.py:115
  41.2 3.3 all-to-all-start.2
  44.5 8.0 %select_select_fusion = bf16[4,144,7680]{2,1,0:T(8,128)(2,1)} fusion(bf16[4,144,7680]{2,1,0:T(8,128)(2,1)} %bitcast.72, pred[4,144]{1,0:T(4,128)(4,1)S(1)} %get-tuple-element.11, pred[4,144]{1,0:T(4,128)(4,1)S(1)} %get-tuple-element.10), kind=kLoop, calls=%fused_computation.3 | loop fusion | flops 8847360 | bytes 17695872 | tf_op jit(solution)/shard_map/jit(_where)/select_n | solution.py:115
  52.5 5.7 %all-to-all-start = ((bf16[4,144,7680]{2,1,0:T(8,128)(2,1)}), bf16[4,144,7680]{2,1,0:T(8,128)(2,1)}, u32[]{:S(2)}, u32[]{:S(2)}) async-start(bf16[4,144,7680]{2,1,0:T(8,128)(2,1)} %select_select_fusion), calls=%async_computation | async-start | bytes 17694720 | tf_op jit(solution)/shard_map/all_to_all | solution.py:123
  58.3 0.0 all-reduce.2.cloned.1.call-start
  58.4 4.2 %gather_fusion.1 = bf16[576,2560]{1,0:T(8,128)(2,1)} fusion(bf16[240,2560]{1,0:T(8,128)(2,1)S(1)} %copy-done, s32[1024]{0:T(1024)S(1)} %pad_clamp_fusion), kind=kCustom, calls=%fused_computation.1 | custom fusion | bytes 5900544 | tf_op jit(solution)/shard_map/jit(_take)/gather | solution.py:116
  62.6 2.3 select_select_fusion.1
  64.9 0.0 copy-start.5
  64.9 0.2 dynamic-slice_bitcast_fusion
  65.1 0.6 collective-permute-start
  65.6 1.7 collective-permute-start.1
  67.3 1.2 collective-permute-start.2
  68.6 2.0 select_select_fusion.2
  70.6 0.5 broadcast.271
  71.1 0.7 reduce.4
  71.8 0.1 lt.187
  71.9 0.1 fusion.39
  71.9 0.1 reshape.370
  72.0 0.1 eq.91
  72.1 99.6 %collective-permute-done = bf16[1,1,144,2560]{3,2,0,1:T(8,128)(2,1)} collective-permute-done((bf16[1,1,144,2560]{3,2,0,1:T(8,128)(2,1)S(1)}, bf16[1,1,144,2560]{3,2,0,1:T(8,128)(2,1)}, u32[]{:S(2)}, u32[]{:S(2)}) %collective-permute-start) | collective-permute-done | bytes 737312 | tf_op jit(solution)/shard_map/ppermute | solution.py:30
  171.8 2.0 constant_dynamic-update-slice_fusion.2
  173.8 2.0 constant_dynamic-update-slice_fusion.1
  175.8 10.0 %collective-permute-done.2 = bf16[1,1,144,2560]{3,2,0,1:T(8,128)(2,1)S(1)} collective-permute-done((bf16[1,1,144,2560]{3,2,0,1:T(8,128)(2,1)S(1)}, bf16[1,1,144,2560]{3,2,0,1:T(8,128)(2,1)S(1)}, u32[]{:S(2)}, u32[]{:S(2)}) %collective-permute-start.2) | collective-permute-done | bytes 737312 | tf_op jit(solution)/shard_map/ppermute | solution.py:30
  185.8 0.9 constant_dynamic-update-slice_fusion
  186.7 2.9 fusion.46
  189.6 0.5 convolution_bitcast_fusion.1
  190.1 4.0 %slice_bitcast_fusion.2 = (bf16[12,6,20,8,128]{4,3,2,1,0:T(8,128)(2,1)S(1)}, bf16[12,6,20,8,128]{4,3,2,1,0:T(8,128)(2,1)S(1)}, bf16[12,6,20,8,128]{4,3,2,1,0:T(8,128)(2,1)S(1)}) fusion(bf16[12,48,7680]{2,1,0:T(8,128)(2,1)} %bitcast.5), kind=kLoop, calls=%fused_computation.23 | loop fusion | bytes 17694720
  194.1 1.7 fusion
  195.8 0.1 broadcast_add_fusion
  195.9 2.0 convert_bitcast_fusion
  197.9 2.6 copy.30
  200.5 34.1 %all-gather.2.cloned.1.call-done = bf16[2560,2560]{1,0:T(8,128)(2,1)} async-done(((bf16[2560,640]{1,0:T(8,128)(2,1)}), bf16[2560,2560]{1,0:T(8,128)(2,1)}) %all-gather.2.cloned.1.call-update) | async-done | bytes 13107216 | tf_op jit(solution)/shard_map/all_gather | solution.py:66
  234.6 12.3 %multiply_convert_fusion = bf16[576,2560]{1,0:T(8,128)(2,1)S(1)} fusion(bf16[576,2560]{1,0:T(8,128)(2,1)} %bitcast.70, bf16[2560,2560]{1,0:T(8,128)(2,1)} %all-gather.2.cloned.1.call-done, bf16[72,8,20,128]{3,2,1,0:T(8,128)(2,1)} %bitcast.75, f32[576]{0:T(1024)S(1)} %reshape.370), kind=kOutput, calls=%fused_computation.4 | convolution fusion | flops 7555645440 | bytes 21956864 | tf_op jit(solution)/shard_map/dot_general | solution.py:64
  246.9 0.0 copy-start.4
  246.9 0.9 fusion.45
  247.8 0.0 copy-start.1
  247.8 0.5 convolution_bitcast_fusion
  248.3 0.2 copy-done.4
  248.5 0.7 pad_maximum_fusion
  249.2 0.0 all-reduce.2.cloned.1.call-update
  249.2 92.1 %all-reduce.2.cloned.1.call-done = f32[2,2560,8]{1,2,0:T(8,128)} async-done(((f32[2,2560,8]{1,2,0:T(8,128)}), f32[2,2560,8]{1,2,0:T(8,128)}) %all-reduce.2.cloned.1.call-update) | async-done | bytes 163856 | tf_op jit(solution)/shard_map/psum | solution.py:133
  341.3 1.6 copy.65
  (27 shorter events, 0.1 us)
Async XLA Ops:
  7.2 51.2 %copy-start = (bf16[240,2560]{1,0:T(8,128)(2,1)S(1)}, bf16[240,2560]{1,0:T(8,128)(2,1)}, u32[]{:S(2)}) copy-start(bf16[240,2560]{1,0:T(8,128)(2,1)} %param.8) | copy-start | bytes 3686404
  7.2 0.8 copy-start.7
  7.2 0.9 copy-start.8
  7.2 6.2 %copy-start.2 = (s32[240]{0:T(256)S(1)}, s32[240]{0:T(256)}, u32[]{:S(2)}) copy-start(s32[240]{0:T(256)} %param.11) | copy-start | bytes 2884
  7.2 227.4 %all-gather.2.cloned.1.call-start = ((), (), s32[]{:S(2)}) async-start(), calls=%async_computation.3 | async-start | bytes 16384000 | tf_op jit(solution)/shard_map/all_gather | solution.py:66
  9.2 32.0 %all-to-all-start.1 = ((s32[4,1,3]{2,1,0:T(1,128)}), s32[4,1,3]{2,1,0:T(1,128)S(1)}, u32[]{:S(2)}, u32[]{:S(2)}) async-start(s32[4,1,3]{2,1,0:T(1,128)} %copy.27), calls=%async_computation.1 | async-start | bytes 4096 | tf_op jit(solution)/shard_map/all_to_all | solution.py:120
  41.2 11.3 %all-to-all-start.2 = ((s32[4,1,144]{2,1,0:T(1,128)}), s32[4,1,144]{2,1,0:T(1,128)S(1)}, u32[]{:S(2)}, u32[]{:S(2)}) async-start(s32[4,1,144]{2,1,0:T(1,128)} %copy.31), calls=%async_computation.2 | async-start | bytes 8192 | tf_op jit(solution)/shard_map/all_to_all | solution.py:119
  52.5 137.5 %all-to-all-start = ((bf16[4,144,7680]{2,1,0:T(8,128)(2,1)}), bf16[4,144,7680]{2,1,0:T(8,128)(2,1)}, u32[]{:S(2)}, u32[]{:S(2)}) async-start(bf16[4,144,7680]{2,1,0:T(8,128)(2,1)} %select_select_fusion), calls=%async_computation | async-start | bytes 17694720 | tf_op jit(solution)/shard_map/all_to_all | solution.py:123
  58.3 283.0 %all-reduce.2.cloned.1.call-start = ((), (), s32[]{:S(2)}) async-start(), calls=%async_computation.4 | async-start | bytes 327680 | tf_op jit(solution)/shard_map/psum | solution.py:133
  64.9 3.7 %copy-start.5 = (bf16[576,2560]{1,0:T(8,128)(2,1)S(1)}, bf16[576,2560]{1,0:T(8,128)(2,1)}, u32[]{:S(2)}) copy-start(bf16[576,2560]{1,0:T(8,128)(2,1)} %gather_fusion.1) | copy-start | bytes 8847364
  65.1 106.7 %collective-permute-start = (bf16[1,1,144,2560]{3,2,0,1:T(8,128)(2,1)S(1)}, bf16[1,1,144,2560]{3,2,0,1:T(8,128)(2,1)}, u32[]{:S(2)}, u32[]{:S(2)}) collective-permute-start(bf16[1,1,144,2560]{3,2,0,1:T(8,128)(2,1)S(1)} %get-tuple-element.9), channel_id=1, source_target_pairs={{0,4},{4,8},{8,12},{12,0},{1,5},{5,9},{9,13},{13,1},{2,6},{6,10},{... | collective-permute-start | bytes 2211848 | tf_op jit(solution)/shard_map/ppermute | solution.py:30
  65.6 108.1 %collective-permute-start.1 = (bf16[1,1,144,2560]{3,2,0,1:T(8,128)(2,1)S(1)}, bf16[1,1,144,2560]{3,2,0,1:T(8,128)(2,1)}, u32[]{:S(2)}, u32[]{:S(2)}) collective-permute-start(bf16[1,1,144,2560]{3,2,0,1:T(8,128)(2,1)S(1)} %get-tuple-element.8), channel_id=1, source_target_pairs={{0,8},{4,12},{8,0},{12,4},{1,9},{5,13},{9,1},{13,5},{2,10},{6,14},... | collective-permute-start | bytes 2211848 | tf_op jit(solution)/shard_map/ppermute | solution.py:30
  67.3 118.5 %collective-permute-start.2 = (bf16[1,1,144,2560]{3,2,0,1:T(8,128)(2,1)S(1)}, bf16[1,1,144,2560]{3,2,0,1:T(8,128)(2,1)S(1)}, u32[]{:S(2)}, u32[]{:S(2)}) collective-permute-start(bf16[1,1,144,2560]{3,2,0,1:T(8,128)(2,1)S(1)} %get-tuple-element.7), channel_id=1, source_target_pairs={{0,12},{4,0},{8,4},{12,8},{1,13},{5,1},{9,5},{13,9},{2,14},{6,2},{... | collective-permute-start | bytes 2211848 | tf_op jit(solution)/shard_map/ppermute | solution.py:30
  70.6 116.1 %copy-start.6 = (bf16[2,2560,8]{1,2,0:T(8,128)(2,1)S(1)}, bf16[2,2560,8]{1,2,0:T(8,128)(2,1)}, u32[]{:S(2)}) copy-start(bf16[2,2560,8]{1,2,0:T(8,128)(2,1)} %param.10) | copy-start | bytes 245764
  186.7 2.9 copy-start.3
  246.9 1.6 copy-start.4
  247.8 95.1 %copy-start.1 = (bf16[240,2560]{1,0:T(8,128)(2,1)S(1)}, bf16[240,2560]{1,0:T(8,128)(2,1)}, u32[]{:S(2)}) copy-start(bf16[240,2560]{1,0:T(8,128)(2,1)} %param.8) | copy-start | bytes 3686404
Sparse Core Ops, SparseCore 0:
  9.6 224.9 all-gather.1
  249.3 91.9 all-reduce.1
